TPU v7x, 512 devices: a whole 4x8x8 slice. The times are simulated.
512 devices in a mesh: pair: 16 (over x, y_hi, core), virt: 32 (over z, y_lo).
Axes of the slice: x: 4, y: 8 (y_hi: 2, y_lo: 4; y = y_hi * 4 + y_lo), z: 8, core: 2. Of those that a mesh axis runs over, the one named last changes fastest.
Arguments:
- amplitudes: bfloat16 [16384, 1024], P(('pair', 'virt')), may hold values from -6 to 6
- integrals: bfloat16 [1024, 65536], P('pair', 'virt'), may hold values from -0.1875 to 0.1875
- amp_mask: int32 [256, 16], P('pair'), may hold values from 0 to 1, as said below
- integral_mask: int32 [16, 1024], P('pair', 'virt'), may hold values 0 or 1
Outputs:
- ladder: bfloat16 [16384, 65536], P('pair', 'virt')
Inputs may be any that keep to these rules, and one draw needn't show every extreme that they name: `amp_mask`: 0 or 1. For every block of 16 consecutive ij tiles, the cd tiles that hold nonzeros lie within one cyclic window of cd tiles common to the block, whose length may differ from block to block.
All inputs are finite; a program needn't handle non-finite values. No bound on the sum of `integral_mask` on one device may be relied on, other than what follows from the above.
Results may differ from a plain program's by a relative error of at most 0.001.
Values may be sent and summed in bfloat16 or wider, within the bound.
No kernel may reach another device: no remote copies, remote signals or barrier semaphores. Data moves between devices by JAX's collectives and lax.ppermute only.
A program may use at most 64 MiB of HBM per device.

v0:
```python
import jax
import jax.numpy as jnp
from jax import lax
from jax.sharding import PartitionSpec as P

TILE = 64


def widened_mask(values, mask):
    tile_rows, tile_columns = mask.shape
    shaped = values.reshape(tile_rows, TILE, tile_columns, TILE)
    return (shaped * mask.astype(values.dtype)[:, None, :, None]).reshape(values.shape)


def on_device(amplitudes, integrals, amp_mask, integral_mask):
    full_amp = lax.all_gather(amplitudes, "virt", axis=0, tiled=True)
    masked_amp = widened_mask(full_amp, amp_mask)
    own_panel = widened_mask(integrals, integral_mask)
    whole_panel = lax.all_gather(own_panel, "pair", axis=0, tiled=True)
    result = jnp.dot(masked_amp, whole_panel, preferred_element_type=jnp.float32)
    return result.astype(jnp.bfloat16)


def solution(mesh):
    in_specs = (P(("pair", "virt"), None), P("pair", "virt"), P("pair", None), P("pair", "virt"))
    out_specs = P("pair", "virt")
    return jax.shard_map(
        on_device, mesh=mesh, in_specs=in_specs, out_specs=out_specs, check_vma=False
    )
```

profile of v0, /device:TPU:1, one launch (start us, length us, event | category | flops | bytes accessed | tf_op | source)
XLA Modules:
  0.0 274.7 jit_solution(16566469928729654126)
XLA Ops:
  6.5 0.0 all-gather.3.cloned.1.call-start
  6.5 0.7 all-gather.3.cloned.1.call-update
  7.3 0.0 all-gather.5.cloned.1.call-start
  7.3 0.7 convert_bitcast_fusion
  8.0 0.1 mul.32
  8.0 0.1 mul.33
  8.1 1.7 broadcast_multiply_fusion
  9.8 0.0 all-gather.5.cloned.1.call-update
  9.8 0.7 convert_element_type.9
  10.5 2.6 mul.28
  13.1 5.5 %mul.29 = bf16[1024,1024]{1,0:T(8,128)(2,1)S(1)} reshape(bf16[16,64,16,64]{3,2,1,0:T(8,128)(2,1)} %mul.28) | data formatting | bytes 4194304 | tf_op jit(solution)/shard_map/mul | solution.py:12
  18.6 134.1 %all-gather.3.cloned.1.call-done = bf16[1024,1024]{1,0:T(8,128)(2,1)} async-done(((bf16[32,1024]{1,0:T(8,128)(2,1)}), bf16[1024,1024]{1,0:T(8,128)(2,1)}) %all-gather.3.cloned.1.call-update) | async-done | bytes 2097168 | tf_op jit(solution)/shard_map/all_gather | solution.py:16
  152.8 105.7 %all-gather.5.cloned.1.call-done = bf16[1024,2048]{1,0:T(8,128)(2,1)} async-done(((bf16[64,2048]{1,0:T(8,128)(2,1)}), bf16[1024,2048]{1,0:T(8,128)(2,1)}) %all-gather.5.cloned.1.call-update) | async-done | bytes 4194320 | tf_op jit(solution)/shard_map/all_gather | solution.py:19
  258.5 9.3 %convolution_convert_fusion = bf16[1024,2048]{1,0:T(8,128)(2,1)} fusion(bf16[1024,2048]{1,0:T(8,128)(2,1)} %all-gather.5.cloned.1.call-done, bf16[1024,1024]{1,0:T(8,128)(2,1)} %all-gather.3.cloned.1.call-done, bf16[1024,1024]{1,0:T(8,128)(2,1)S(1)} %mul.29), kind=kOutput, calls=%fused_computation | convolution fusion | flops 4298113024 | bytes 12582912 | tf_op jit(solution)/shard_map/dot_general | solution.py:20
Async XLA Ops:
  6.5 146.2 %all-gather.3.cloned.1.call-start = ((), (), s32[]{:S(2)}) async-start(), calls=%async_computation | async-start | bytes 2162688 | tf_op jit(solution)/shard_map/all_gather | solution.py:16
  7.3 251.2 %all-gather.5.cloned.1.call-start = ((), (), s32[]{:S(2)}) async-start(), calls=%async_computation.1 | async-start | bytes 4456448 | tf_op jit(solution)/shard_map/all_gather | solution.py:19
Sparse Core Ops, SparseCore 0:
  9.4 143.3 all-gather.2
  156.0 102.4 all-gather.4
where the time goes:
time: 275 us
  waiting for transfers between devices  241 us (88%)
  between operations  13.4 us (5%)
  matrix products  9.34 us (3%)
  local copies, waits for them, and re-layouts  8.26 us (3%)
  other arithmetic  3.02 us (1%)
    all_gather x1, waiting for transfers between devices, on_device(): full_amp = lax.all_gather(amplitudes, 'virt', axis=0, tiled=True)  134 us
    all_gather x1, waiting for transfers between devices, on_device(): whole_panel = lax.all_gather(own_panel, 'pair', axis=0, tiled=True)  106 us
    dot_general x1, matrix products, on_device(): jnp.dot(masked_amp, whole_panel, preferred_element_type=jnp.float32)  9.34 us
    mul x4, local copies, waits for them, and re-layouts, widened_mask(): shaped * mask.astype(values.dtype)[:, None, :, None]  8.26 us
  transfers between devices with their start and end apart: 2, of which 2 were waited for; matrix products, arithmetic and copies ran while one was open for 4% of the time, Pallas kernels for 0%

commit v1 on v0

--- a/solution.py
+++ b/solution.py
@@ -16,7 +16,9 @@
     full_amp = lax.all_gather(amplitudes, "virt", axis=0, tiled=True)
     masked_amp = widened_mask(full_amp, amp_mask)
     own_panel = widened_mask(integrals, integral_mask)
-    whole_panel = lax.all_gather(own_panel, "pair", axis=0, tiled=True)
+    whole_panel = jnp.concatenate(
+        lax.all_to_all(jnp.stack([own_panel] * lax.axis_size("pair")), "pair", 0, 0), axis=0
+    )
     result = jnp.dot(masked_amp, whole_panel, preferred_element_type=jnp.float32)
     return result.astype(jnp.bfloat16)
 

time: 275 us -> 221 us (0.80)
  the two profiles are of different devices: /device:TPU:1 before, /device:TPU:2 now
where the time goes in v1:
time: 221 us; the launch traced here: 220 us
  waiting for transfers between devices  175 us (79%)
  between operations  13.4 us (6%)
  local copies, waits for them, and re-layouts  10.8 us (5%)
  starting transfers between devices  10.3 us (5%)
  matrix products  9.34 us (4%)
    all_gather x1, waiting for transfers between devices, on_device(): full_amp = lax.all_gather(amplitudes, 'virt', axis=0, tiled=True)  174 us
    all_to_all x1, starting transfers between devices, on_device(): lax.all_to_all(jnp.stack([own_panel] * lax.axis_size('pair')), 'pair', 0, 0)  10.3 us
    dot_general x1, matrix products, on_device(): jnp.dot(masked_amp, whole_panel, preferred_element_type=jnp.float32)  9.34 us
    mul x4, local copies, waits for them, and re-layouts, widened_mask(): shaped * mask.astype(values.dtype)[:, None, :, None]  8.22 us
  transfers between devices with their start and end apart: 2, of which 1 were waited for; matrix products, arithmetic and copies ran while one was open for 4% of the time, Pallas kernels for 0%

profile of v1, /device:TPU:2, one launch (start us, length us, event | category | flops | bytes accessed | tf_op | source)
XLA Modules:
  0.0 220.2 jit_solution(8721759565722545066)
XLA Ops:
  6.5 0.7 convert_bitcast_fusion
  7.2 0.1 mul.33
  7.3 0.1 mul.34
  7.4 1.0 broadcast_multiply_fusion
  8.3 2.5 %stack.3 = bf16[16,64,2048]{2,1,0:T(8,128)(2,1)} broadcast(bf16[64,2048]{1,0:T(8,128)(2,1)S(1)} %broadcast_multiply_fusion), dimensions={1,2} | broadcast | bytes 4456448 | tf_op jit(solution)/shard_map/stack | solution.py:20
  10.9 0.0 copy-start
  10.9 10.3 %all-to-all-start = ((bf16[16,64,2048]{2,1,0:T(8,128)(2,1)}), bf16[16,64,2048]{2,1,0:T(8,128)(2,1)}, u32[]{:S(2)}, u32[]{:S(2)}) async-start(bf16[16,64,2048]{2,1,0:T(8,128)(2,1)} %stack.3), calls=%async_computation | async-start | bytes 8388608 | tf_op jit(solution)/shard_map/all_to_all | solution.py:20
  21.2 0.0 all-gather.2.cloned.1.call-start
  21.2 0.7 all-gather.2.cloned.1.call-update
  21.9 0.0 copy-done
  21.9 2.6 %mul.29 = bf16[16,64,16,64]{3,2,1,0:T(8,128)(2,1)} broadcast(bf16[16,16]{1,0:T(8,128)(2,1)S(1)} %convert_element_type.9), dimensions={0,2} | broadcast | bytes 2097664 | tf_op jit(solution)/shard_map/mul | solution.py:12
  24.5 5.5 %mul.30 = bf16[1024,1024]{1,0:T(8,128)(2,1)S(1)} reshape(bf16[16,64,16,64]{3,2,1,0:T(8,128)(2,1)} %mul.29) | data formatting | bytes 4194304 | tf_op jit(solution)/shard_map/mul | solution.py:12
  30.0 174.0 %all-gather.2.cloned.1.call-done = bf16[1024,1024]{1,0:T(8,128)(2,1)} async-done(((bf16[32,1024]{1,0:T(8,128)(2,1)}), bf16[1024,1024]{1,0:T(8,128)(2,1)}) %all-gather.2.cloned.1.call-update) | async-done | bytes 2097168 | tf_op jit(solution)/shard_map/all_gather | solution.py:16
  204.0 0.0 all-to-all-done
  204.0 9.3 %convolution_convert_fusion = bf16[1024,2048]{1,0:T(8,128)(2,1)} fusion(bf16[1024,2048]{1,0:T(8,128)(2,1)} %bitcast.1, bf16[1024,1024]{1,0:T(8,128)(2,1)} %all-gather.2.cloned.1.call-done, bf16[1024,1024]{1,0:T(8,128)(2,1)S(1)} %mul.30), kind=kOutput, calls=%fused_computation | convolution fusion | flops 4298113024 | bytes 12582912 | tf_op jit(solution)/shard_map/dot_general | solution.py:22
  (1 shorter events, 0.0 us)
Async XLA Ops:
  10.9 11.0 %copy-start = (s32[16,16]{1,0:T(8,128)S(1)}, s32[16,16]{1,0:T(8,128)}, u32[]{:S(2)}) copy-start(s32[16,16]{1,0:T(8,128)} %param.6) | copy-start | bytes 3076
  10.9 193.2 %all-to-all-start = ((bf16[16,64,2048]{2,1,0:T(8,128)(2,1)}), bf16[16,64,2048]{2,1,0:T(8,128)(2,1)}, u32[]{:S(2)}, u32[]{:S(2)}) async-start(bf16[16,64,2048]{2,1,0:T(8,128)(2,1)} %stack.3), calls=%async_computation | async-start | bytes 8388608 | tf_op jit(solution)/shard_map/all_to_all | solution.py:20
  21.2 182.9 %all-gather.2.cloned.1.call-start = ((), (), s32[]{:S(2)}) async-start(), calls=%async_computation.1 | async-start | bytes 2162688 | tf_op jit(solution)/shard_map/all_gather | solution.py:16
Sparse Core Ops, SparseCore 0:
  24.1 179.9 all-gather.1
